TPU v7x, 256 devices: a whole 4x4x8 slice. The times are simulated.
256 devices in a mesh: seq: 32 (over z, y), exp: 8 (over x, core).
Axes of the slice: x: 4, y: 4, z: 8, core: 2. Of those that a mesh axis runs over, the one named last changes fastest.
Arguments:
- residual: bfloat16 [4096, 6144], P('exp', 'seq'), may hold values from -8 to 8
- query: bfloat16 [4096, 8192], P('seq', 'exp'), may hold values from -6 to 6
- key_in: bfloat16 [4096, 8192], P('seq', 'exp'), may hold values from -6 to 6
- value_in: bfloat16 [4096, 8192], P('seq', 'exp'), may hold values from -0.75 to 0.75
- gate_in: bfloat16 [4096, 8192], P('seq', 'exp'), may hold values from -6 to 6
- log_decay: float32 [4096, 64], P('seq', 'exp'), may hold values from -2 to 0
- state_in: float32 [64, 128, 128], P('exp'), may hold values from -12 to 12
- attn_gain: float32 [8192], P('exp'), may hold values from 0.1 to 1.9
- w_out: bfloat16 [8192, 6144], P('exp', 'seq'), may hold values from -0.0625 to 0.0625
- moe_gain: float32 [6144], P('seq'), may hold values from 0.1 to 1.9
- router: float32 [6144, 32], P('seq'), may hold values from -0.078125 to 0.078125
- w_gate: bfloat16 [8, 9216, 6144], P('exp', 'seq'), may hold values from -0.078125 to 0.078125
- w_up: bfloat16 [8, 9216, 6144], P('exp', 'seq'), may hold values from -0.078125 to 0.078125
- w_down: bfloat16 [8, 9216, 6144], P('exp', None, 'seq'), may hold values from -0.125 to 0.125
- expert_ids: int32 [4096, 2], P('exp'), may hold values from 0 to 31, all different within a row; in each aligned block of 512 rows (0 to 511, 512 to 1023, ...) at most 40 rows name the same one
- keep_counts: int32 [32], replicated, may hold values from 64 to 319
Outputs:
- layer_out: bfloat16 [4096, 6144], P('exp', 'seq')
- final_state: float32 [64, 128, 128], P('exp', 'seq')
Inputs may be any that keep to these rules, and one draw needn't show every extreme that they name: `expert_ids`: each row names 2 different experts. Among the rows of one device no expert is named more than 40 times, a bound that some block reaches.
All inputs are finite; a program needn't handle non-finite values.
Results may differ from a plain program's by a relative error of at most 0.014.
Values may be sent and summed in bfloat16 or wider, within the bound.
A program may use at most 128 MiB of HBM per device.

v0:
```python
import jax
import jax.numpy as jnp
from jax import lax
from jax.sharding import PartitionSpec as P

D = 6144


epsilon = 1e-05
highest = lax.Precision.HIGHEST


def entering(x, axis, join, neutral):
    place = lax.axis_index(axis)
    gathered = jax.tree.map(
        lambda a, kind: lax.all_gather(a.astype(kind), axis), x, (jnp.bfloat16, jnp.bfloat16)
    )
    state = jax.tree.map(lambda a, e: jnp.zeros_like(a) + jnp.asarray(e, a.dtype), x, neutral)

    def one(lap, state):
        return join(
            state,
            jax.tree.map(
                lambda a, own: lax.dynamic_index_in_dim(a, lap, 0, False).astype(own.dtype),
                gathered,
                x,
            ),
        )

    return lax.fori_loop(0, place, one, state)


def broadcast(value, axis, source):
    kept = jnp.where(lax.axis_index(axis) == source, value, 0).astype(value.dtype)
    return lax.psum(kept, axis)


def entering_2(part, axis, combine, identity):
    place = lax.axis_index(axis)
    gathered = lax.all_gather(part, axis)
    state = jnp.zeros_like(part) + jnp.asarray(identity, part.dtype)

    def one(lap, state):
        return combine(state, lax.dynamic_index_in_dim(gathered, lap, 0, False))

    return lax.fori_loop(0, place, one, state)


def block_terms(act_query, act_key, val_rows, log_rows):
    running_log = jnp.cumsum(log_rows, axis=0)
    block_log = running_log[-1]
    length = log_rows.shape[0]
    causal_mask = (jnp.arange(length)[:, None] >= jnp.arange(length)[None, :])[None]
    flipped = jnp.transpose(running_log)
    log_gap = flipped[:, :, None] - flipped[:, None, :]
    decay_rows = jnp.where(causal_mask, jnp.exp(jnp.where(causal_mask, log_gap, 0.0)), 0.0)
    scores = jnp.einsum("thd,shd->hts", act_query, act_key, precision=highest)
    local_part = jnp.einsum("hts,shd->thd", scores * decay_rows, val_rows, precision=highest)
    tail_decay = jnp.exp(block_log[None, :] - running_log)
    update = jnp.einsum(
        "shd,she->hde", act_key * tail_decay[:, :, None], val_rows, precision=highest
    )
    return (local_part, running_log, block_log, update)


def from_state(act_query, running_log, state_carry):
    return jnp.einsum(
        "thd,hde->the", act_query * jnp.exp(running_log)[:, :, None], state_carry, precision=highest
    )


def join_states(earlier, later_part):
    return (
        earlier[0] + later_part[0],
        jnp.exp(later_part[0])[:, None, None] * earlier[1] + later_part[1],
    )


def add_counts(earlier, later_counts):
    return earlier + later_counts


def local(
    residual,
    query,
    key_in,
    value_in,
    gate_in,
    log_decay,
    state_in,
    attn_gain,
    w_out,
    moe_gain,
    router,
    w_gate,
    w_up,
    w_down,
    expert_ids,
    keep_counts,
):
    tok_rows, head_width = query.shape
    head_count = log_decay.shape[1]
    head_size = head_width // head_count
    act_query = jax.nn.silu(query.astype(jnp.float32)).reshape(tok_rows, head_count, head_size)
    act_key = jax.nn.silu(key_in.astype(jnp.float32)).reshape(tok_rows, head_count, head_size)
    val_rows = value_in.astype(jnp.float32).reshape(tok_rows, head_count, head_size)
    local_part, running_log, block_log, update = block_terms(
        act_query, act_key, val_rows, log_decay
    )
    segments = lax.axis_size("seq")
    position = lax.axis_index("seq")
    row_share = head_size // segments
    identity_pair = (jnp.zeros_like(block_log), jnp.zeros_like(update))
    before_log, before_state = entering((block_log, update), "seq", join_states, identity_pair)
    incoming = jnp.exp(before_log)[:, None, None] * state_in + before_state
    through = jnp.exp(block_log)[:, None, None] * incoming + update
    last_whole = broadcast(through.astype(jnp.bfloat16), "seq", segments - 1).astype(through.dtype)
    final_rows = lax.dynamic_slice_in_dim(last_whole, position * row_share, row_share, 1)
    outputs = local_part + from_state(act_query, running_log, incoming)
    square_mean = jnp.mean(outputs * outputs, axis=2, keepdims=True)
    normed = outputs * lax.rsqrt(square_mean + epsilon) * attn_gain.reshape(head_count, head_size)
    heads_mixed = (
        normed.reshape(tok_rows, head_width) * jax.nn.sigmoid(gate_in.astype(jnp.float32))
    ).astype(jnp.bfloat16)
    gathered = lax.all_gather(heads_mixed, "seq", axis=0, tiled=True)
    block_rows = residual.shape[0]
    projected = lax.psum_scatter(
        jnp.dot(gathered, w_out, preferred_element_type=jnp.float32).astype(jnp.bfloat16),
        "exp",
        scatter_dimension=0,
        tiled=True,
    ).astype(jnp.float32)
    after_attn = residual.astype(jnp.float32) + projected
    experts_all = router.shape[1]
    logit_part = jnp.dot(after_attn * moe_gain, router, precision=highest)
    choose = (
        expert_ids[:, :, None] == jnp.arange(experts_all, dtype=jnp.int32)[None, None, :]
    ).astype(jnp.float32)
    chosen_part = jnp.einsum("tke,te->tk", choose, logit_part, precision=highest)
    squares, chosen = lax.psum((jnp.sum(after_attn * after_attn, axis=1), chosen_part), "seq")
    inv_rms = lax.rsqrt(squares / D + epsilon)
    chosen = chosen * inv_rms[:, None]
    gate_probs = jnp.stack(
        [jax.nn.sigmoid(chosen[:, 0] - chosen[:, 1]), jax.nn.sigmoid(chosen[:, 1] - chosen[:, 0])],
        axis=1,
    )
    routed_in = (after_attn * inv_rms[:, None] * moe_gain).astype(jnp.bfloat16)
    lanes = lax.axis_size("exp")
    window = w_gate.shape[0] * lanes
    capacity = 5 * block_rows * lanes // (2 * lanes * experts_all)
    top_count = expert_ids.shape[1]
    flat_ids = expert_ids.reshape(block_rows * top_count)
    onehot = (flat_ids[:, None] == jnp.arange(window, dtype=jnp.int32)[None, :]).astype(jnp.int32)
    local_rank = jnp.sum((jnp.cumsum(onehot, axis=0) - onehot) * onehot, axis=1)
    before = entering_2(jnp.sum(onehot, axis=0), "exp", add_counts, jnp.zeros((window,), jnp.int32))
    global_rank = local_rank + jnp.sum(before[None, :] * onehot, axis=1)
    limits = jnp.sum(keep_counts[None, :window] * onehot, axis=1)
    is_kept = (flat_ids < window) & (global_rank < limits)
    slot_hot = ((local_rank[:, None] == jnp.arange(capacity)[None, :]) & is_kept[:, None]).astype(
        jnp.int32
    )
    assign_int = onehot[:, :, None] * slot_hot[:, None, :]
    assign_table = assign_int.astype(jnp.bfloat16)
    token_table = jnp.sum(
        assign_int.reshape(block_rows, top_count, window, capacity), axis=1
    ).astype(jnp.bfloat16)
    sending = jnp.einsum(
        "tec,td->ecd", token_table, routed_in, preferred_element_type=jnp.float32
    ).astype(jnp.bfloat16)
    arrived = lax.all_to_all(sending, "exp", split_axis=0, concat_axis=1, tiled=True)
    contract_dims = (((1,), (1,)), ((), ()))
    portion = lax.all_gather(arrived, "seq", axis=2, tiled=True)
    gate_cols = w_gate[0]
    up_cols = w_up[0]
    gate_add = lax.dot_general(
        portion[0], gate_cols, contract_dims, preferred_element_type=jnp.float32
    )
    up_add = lax.dot_general(portion[0], up_cols, contract_dims, preferred_element_type=jnp.float32)
    hidden = (jax.nn.silu(gate_add) * up_add).astype(jnp.bfloat16)
    down_rows = w_down[0]
    result = jnp.dot(
        lax.all_gather(hidden, "seq", axis=1, tiled=True),
        down_rows,
        preferred_element_type=jnp.float32,
    )
    expert_out = result.astype(jnp.bfloat16)[None]
    returned = lax.all_to_all(expert_out, "exp", split_axis=1, concat_axis=0, tiled=True)
    picked = jnp.einsum(
        "aec,ecd->ad", assign_table, returned, preferred_element_type=jnp.float32
    ).reshape(block_rows, top_count, -1)
    weight = jnp.where(is_kept.reshape(block_rows, top_count), gate_probs, 0.0)
    expert_sum = jnp.sum(picked * weight[:, :, None], axis=1)
    return ((after_attn + expert_sum).astype(jnp.bfloat16), final_rows)


def solution(mesh):
    in_specs = (
        P("exp", "seq"),
        P("seq", "exp"),
        P("seq", "exp"),
        P("seq", "exp"),
        P("seq", "exp"),
        P("seq", "exp"),
        P("exp", None, None),
        P("exp"),
        P("exp", "seq"),
        P("seq"),
        P("seq", None),
        P("exp", "seq", None),
        P("exp", "seq", None),
        P("exp", None, "seq"),
        P("exp", None),
        P(),
    )
    out_specs = (P("exp", "seq"), P("exp", "seq", None))
    return jax.shard_map(local, mesh=mesh, in_specs=in_specs, out_specs=out_specs, check_vma=False)
```

profile of v0, /device:TPU:1, one launch (start us, length us, event | category | flops | bytes accessed | tf_op | source)
XLA Modules:
  0.0 767.0 jit_solution(17127196625241131130)
XLA Ops:
  15.4 2.1 copy.145
  17.5 2.4 fusion.64
  21.5 36.3 %all-gather.2 = bf16[32,1,8]{2,1,0:T(2,128)(2,1)S(1)} all-gather(bf16[1,1,8]{2,1,0:T(2,128)(2,1)S(1)} %convert_bitcast_fusion), channel_id=1, replica_groups=mesh['seq'=32,'exp'=8] {'seq'}, dimensions={0}, use_global_device_ids=true | all-gather | bytes 528 | tf_op jit(solution)/shard_map/all_gather | solution.py:16
  62.9 58.1 %all-gather.14.cloned.1.call-done = bf16[256,128,128]{2,1,0:T(8,128)(2,1)} async-done(((bf16[8,128,128]{2,1,0:T(8,128)(2,1)}), bf16[256,128,128]{2,1,0:T(8,128)(2,1)}) %all-gather.14.cloned.1.call-update) | async-done | bytes 8388624 | tf_op jit(solution)/shard_map/all_gather | solution.py:16
  121.9 2.7 multiply_reduce_fusion.1
  125.7 2.0 copy.125
  129.8 157.0 %all-gather.8.cloned.1.call-done = bf16[4096,1024]{1,0:T(8,128)(2,1)} async-done(((bf16[128,1024]{1,0:T(8,128)(2,1)}), bf16[4096,1024]{1,0:T(8,128)(2,1)}) %all-gather.8.cloned.1.call-update) | async-done | bytes 8388624 | tf_op jit(solution)/shard_map/all_gather | solution.py:125
  286.7 7.5 convolution_convert_fusion
  300.6 9.0 %all-reduce = s32[64]{0:T(128)S(1)} all-reduce(s32[64]{0:T(128)} %dynamic-update-slice), channel_id=3, replica_groups=mesh['seq'=32,'exp'=8] {'exp'}, use_global_device_ids=true, to_apply=%add | all-reduce | flops 64 | bytes 512
  310.8 5.1 reduce-window.6
  329.7 2.2 fusion.42
  331.9 8.9 %fusion.36 = f32[512,2]{1,0:T(8,128)} fusion(f32[512,32]{1,0:T(8,128)S(1)} %fusion.42, s32[512,2]{1,0:T(8,128)} %copy.126), kind=kLoop, calls=%fused_computation.42 | loop fusion | flops 97280 | bytes 73728
  343.0 58.3 %all-reduce.1 = (f32[512]{0:T(512)}, f32[512,2]{0,1:T(2,128)}) all-reduce(f32[512]{0:T(512)S(1)} %multiply_reduce_fusion.2, f32[512,2]{0,1:T(2,128)S(1)} %copy.141), channel_id=1, replica_groups=mesh['seq'=32,'exp'=8] {'seq'}, use_global_device_ids=true, to_apply=%region_15.16 | all-reduce | flops 1536 | bytes 12288 | tf_op jit(solution)/shard_map/psum | solution.py:140
  405.8 27.6 %all_to_all.24 = bf16[8,40,192]{2,1,0:T(8,128)(2,1)} all-to-all(bf16[8,40,192]{2,1,0:T(8,128)(2,1)S(1)} %convolution_convert_fusion.1), channel_id=1, replica_groups=mesh['seq'=32,'exp'=8] {'exp'}, dimensions={0} | all-to-all | bytes 245760 | tf_op jit(solution)/shard_map/all_to_all | solution.py:170
  435.1 75.1 %all-gather.10.cloned.1.call-done = bf16[1,320,6144]{1,2,0:T(8,128)(2,1)} async-done(((bf16[1,320,192]{1,2,0:T(8,128)(2,1)}), bf16[1,320,6144]{1,2,0:T(8,128)(2,1)}) %all-gather.10.cloned.1.call-update) | async-done | bytes 3932176 | tf_op jit(solution)/shard_map/all_gather | solution.py:172
  510.3 4.5 fusion
  515.1 2.7 fusion.16
  518.6 2.3 fusion.45
  520.8 89.2 %all-gather.12.cloned.1.call-done = bf16[320,9216]{0,1:T(8,128)(2,1)} async-done(((bf16[320,288]{0,1:T(8,128)(2,1)}), bf16[320,9216]{0,1:T(8,128)(2,1)}) %all-gather.12.cloned.1.call-update) | async-done | bytes 5898256 | tf_op jit(solution)/shard_map/all_gather | solution.py:182
  610.1 6.8 fusion.24
  619.2 3.2 reduce.4
  624.2 5.4 all-to-all-start.1
  629.6 122.9 %all-reduce.4.cloned.1.call-done = bf16[8,128,128]{2,1,0:T(8,128)(2,1)} async-done(((bf16[8,128,128]{2,1,0:T(8,128)(2,1)}), bf16[8,128,128]{2,1,0:T(8,128)(2,1)}) %all-reduce.4.cloned.1.call-update) | async-done | bytes 262160 | tf_op jit(solution)/shard_map/psum | solution.py:35
  753.8 2.3 reshape.243
  (95 shorter events, 59.3 us)
Async XLA Ops:
  7.2 503.1 %copy-start = (bf16[1,288,6144]{2,1,0:T(8,128)(2,1)S(1)}, bf16[1,288,6144]{2,1,0:T(8,128)(2,1)}, u32[]{:S(2)}) copy-start(bf16[1,288,6144]{2,1,0:T(8,128)(2,1)} %param.31) | copy-start | bytes 10616836
  7.2 113.8 %all-gather.14.cloned.1.call-start = ((), (), s32[]{:S(2)}) async-start(), calls=%async_computation.8 | async-start | bytes 8650752 | tf_op jit(solution)/shard_map/all_gather | solution.py:16
  19.9 266.9 %all-gather.8.cloned.1.call-start = ((), (), s32[]{:S(2)}) async-start(), calls=%async_computation.3 | async-start | bytes 8650752 | tf_op jit(solution)/shard_map/all_gather | solution.py:125
  59.3 2.0 copy-start.1
  121.9 2.8 copy-start.4
  121.9 3.8 copy-start.5
  129.7 164.6 %copy-start.3 = (s32[512,2]{0,1:T(2,128)S(1)}, s32[512,2]{0,1:T(2,128)}, u32[]{:S(2)}) copy-start(s32[512,2]{0,1:T(2,128)} %param.34) | copy-start | bytes 12292
  129.7 167.7 %copy-start.9 = (u32[256]{0:T(256)S(1)}, u32[256]{0:T(256)}, u32[]{:S(2)}) copy-start(u32[256]{0:T(256)} %constant.77) | copy-start | bytes 3076
  129.7 200.0 %reduce-scatter.2.cloned.1.call-start = ((), (), s32[]{:S(2)}) async-start(), calls=%async_computation.4 | async-start | bytes 1769472 | tf_op jit(solution)/shard_map/reduce_scatter | solution.py:127
  294.3 216.0 %all-gather.10.cloned.1.call-start = ((), (), s32[]{:S(2)}) async-start(), calls=%async_computation.5 | async-start | bytes 4866048 | tf_op jit(solution)/shard_map/all_gather | solution.py:172
  403.5 2.3 copy-start.2
  435.1 175.0 %all-gather.12.cloned.1.call-start = ((), (), s32[]{:S(2)}) async-start(), calls=%async_computation.6 | async-start | bytes 7299072 | tf_op jit(solution)/shard_map/all_gather | solution.py:182
  510.3 4.5 copy-start.7
  510.3 4.9 copy-start.8
  515.1 3.4 copy-start.6
  517.8 234.6 %all-reduce.4.cloned.1.call-start = ((), (), s32[]{:S(2)}) async-start(), calls=%async_computation.7 | async-start | bytes 524288 | tf_op jit(solution)/shard_map/psum | solution.py:35
  624.2 129.6 %all-to-all-start.1 = ((bf16[8,2,3840]{2,1,0:T(2,128)(2,1)}), bf16[8,2,3840]{2,1,0:T(2,128)(2,1)}, u32[]{:S(2)}, u32[]{:S(2)}) async-start(bf16[8,2,3840]{2,1,0:T(2,128)(2,1)} %reshape.242), calls=%async_computation.2 | async-start | bytes 245760 | tf_op jit(solution)/shard_map/all_to_all | solution.py:187
Sparse Core Ops, SparseCore 0:
  20.0 100.9 all-gather.13
  129.8 156.8 all-gather.7
  294.4 30.9 reduce-scatter.1
  435.2 75.0 all-gather.9
  517.9 92.1 all-gather.11
  613.4 138.9 all-reduce.3
where the time goes:
time: 774 us; the launch traced here: 767 us
  waiting for transfers between devices  502 us (65%)
  blocking collectives  131 us (17%)
  other arithmetic  39.8 us (5%)
  local copies, waits for them, and re-layouts  38 us (5%)
  matrix products  34.9 us (5%)
  between operations  15 us (2%)
    all_gather x1, waiting for transfers between devices, local(): gathered = lax.all_gather(heads_mixed, 'seq', axis=0, tiled=True)  157 us
    psum x1, waiting for transfers between devices, broadcast(): return lax.psum(kept, axis)  123 us
    all_gather x1, waiting for transfers between devices, local(): lax.all_gather(hidden, 'seq', axis=1, tiled=True)  89.2 us
    all_gather x1, waiting for transfers between devices, local(): portion = lax.all_gather(arrived, 'seq', axis=2, tiled=True)  75.1 us
    psum x1, blocking collectives, local(): lax.psum((jnp.sum(after_attn * after_attn, axis=1), chosen_part), 'seq')  58.3 us
    all_gather x1, waiting for transfers between devices, entering(): lax.all_gather(a.astype(kind), axis)  58.1 us
    all_gather x1, blocking collectives, entering(): lax.all_gather(a.astype(kind), axis)  36.3 us
    all_to_all x1, blocking collectives, local(): lax.all_to_all(sending, 'exp', split_axis=0, concat_axis=1, tiled=True)  27.6 us
  transfers between devices with their start and end apart: 7, of which 5 were waited for; matrix products, arithmetic and copies ran while one was open for 7% of the time, Pallas kernels for 0%

commit v1 on v0

v1 whole, which is shorter than its diff:
```python
import jax
import jax.numpy as jnp
from jax import lax
from jax.experimental import pallas as pl
from jax.experimental.pallas import tpu as pltpu
from jax.sharding import PartitionSpec as P

f32, bf16 = jnp.float32, jnp.bfloat16
highest = lax.Precision.HIGHEST
epsilon = 1e-05
D = 6144
NS, NE, NY, NZ = 32, 8, 4, 8
HEADS, HD, TOK = 8, 128, 128
COLS = 192
MESH = pl.DeviceIdType.MESH


def silu(v):
    return v / (1.0 + jnp.exp(-v))


def iota(shape, dim):
    return lax.broadcasted_iota(jnp.int32, shape, dim)


def remote(src, dst, send, recv, dev):
    return pltpu.make_async_remote_copy(
        src_ref=src, dst_ref=dst, send_sem=send, recv_sem=recv, device_id=dev, device_id_type=MESH
    )


def enter(s, e):
    barrier = pltpu.get_barrier_semaphore()

    def seq_signal(o, _):
        pl.semaphore_signal(
            barrier, inc=1, device_id=(lax.rem(s + o, NS), e), device_id_type=MESH
        )
        return 0

    def exp_signal(o, _):
        pl.semaphore_signal(
            barrier, inc=1, device_id=(s, lax.rem(e + o, NE)), device_id_type=MESH
        )
        return 0

    lax.fori_loop(1, NS, seq_signal, 0)
    lax.fori_loop(1, NE, exp_signal, 0)
    return barrier


def attention_kernel(
    q_ref, k_ref, v_ref, g_ref, ld_ref, st_ref, gain_ref, w_hbm, res_ref,
    after_ref, fin_ref,
    ldp, lcol, lrow, kbf, upd, ub, rbuf, pref, pbuf, inc, loc, qd,
    wbuf, wcat, act, pb, sb, qb, rs, ysend, yrecv,
    w_local, w_send, w_recv, a_send, a_recv, b_send, b_recv,
    r_send, r_recv, sb_send, sb_recv, rs_send, rs_recv, y_send, y_recv,
):
    s = lax.axis_index("seq")
    e = lax.axis_index("exp")
    y, z = lax.rem(s, NY), s // NY
    c = lax.rem(e, 2)
    barrier = enter(s, e)
    wl = pltpu.make_async_copy(w_hbm, wbuf.at[y], w_local)
    wl.start()

    ldp[...] = jnp.zeros_like(ldp)
    ldp[:, 0:HEADS] = ld_ref[...]
    tri = (iota((TOK, TOK), 0) >= iota((TOK, TOK), 1)).astype(f32)
    run = jnp.dot(tri, ldp[...], preferred_element_type=f32, precision=highest)
    lcol[...] = run
    lrow[...] = run.T
    for h in range(HEADS):
        cols = slice(h * HD, (h + 1) * HD)
        kh = silu(k_ref[:, cols].astype(f32))
        kbf[:, cols] = kh.astype(bf16)
        tail = jnp.exp(lcol[TOK - 1 : TOK, h : h + 1] - lcol[:, h : h + 1])
        kd = (kh * tail).T.astype(bf16)
        upd[cols, :] = jnp.dot(kd, v_ref[:, cols], preferred_element_type=f32)
    total = jnp.broadcast_to(lrow[0:HEADS, TOK - 1 : TOK], (HEADS, HD))
    high = total.astype(bf16).astype(f32)
    logs = jnp.concatenate([high, total - high], axis=0).astype(bf16)
    for d in range(NS):
        rows = [upd[pl.ds(4 * d + r, HEADS, stride=HD), :] for r in range(4)]
        ub[d, 0:32, :] = jnp.concatenate(rows, axis=0).astype(bf16)
        ub[d, 32:48, :] = logs

    pl.semaphore_wait(barrier, NS - 1 + NE - 1)

    def send_a(o, _):
        peer = lax.rem(s + o, NS)
        remote(ub.at[peer], rbuf.at[s], a_send.at[o], a_recv.at[s], (peer, e)).start()
        return 0

    lax.fori_loop(1, NS, send_a, 0)
    rbuf[s] = ub[s]
    y_right, y_left = lax.rem(y + 1, NY), lax.rem(y + NY - 1, NY)
    y_far = lax.rem(y + 2, NY)
    dev_yr, dev_yl = (z * NY + y_right, e), (z * NY + y_left, e)
    w_r = remote(w_hbm, wbuf.at[y], w_send.at[0], w_recv.at[0], dev_yr)
    w_l = remote(w_hbm, wbuf.at[y], w_send.at[1], w_recv.at[1], dev_yl)
    w_r.start()
    w_l.start()

    causal = iota((TOK, TOK), 0) >= iota((TOK, TOK), 1)
    for h in range(HEADS):
        cols = slice(h * HD, (h + 1) * HD)
        qh = silu(q_ref[:, cols].astype(f32))
        lc = lcol[:, h : h + 1]
        gap = lc - lrow[h : h + 1, :]
        decay = jnp.where(causal, jnp.exp(jnp.where(causal, gap, 0.0)), 0.0)
        scores = lax.dot_general(
            qh.astype(bf16), kbf[:, cols], (((1,), (1,)), ((), ())), preferred_element_type=f32
        )
        loc[:, cols] = jnp.dot(
            (scores * decay).astype(bf16), v_ref[:, cols], preferred_element_type=f32
        )
        qd[:, cols] = (qh * jnp.exp(lc)).astype(bf16)

    def wait_a(o, _):
        src = lax.rem(s + o, NS)
        remote(rbuf.at[src], rbuf.at[src], a_send.at[o], a_recv.at[src], (src, e)).wait_recv()
        return 0

    lax.fori_loop(1, NS, wait_a, 0)
    start = jnp.concatenate(
        [st_ref[pl.ds(4 * s + r, HEADS, stride=HD), :] for r in range(4)], axis=0
    )

    def scan(j, state):
        pref[j] = state.astype(bf16)
        piece = rbuf[j].astype(f32)
        dec = jnp.exp(piece[32:40] + piece[40:48])
        return state * jnp.concatenate([dec] * 4, axis=0) + piece[0:32]

    last = lax.fori_loop(0, NS, scan, start)
    for r in range(4):
        for h in range(HEADS):
            fin_ref[h, r : r + 1, :] = last[8 * r + h : 8 * r + h + 1, :]

    def send_b(o, _):
        peer = lax.rem(s + o, NS)
        remote(pref.at[peer], pbuf.at[s], b_send.at[o], b_recv.at[s], (peer, e)).start()
        return 0

    lax.fori_loop(1, NS, send_b, 0)
    pbuf[s] = pref[s]
    half = 512
    remote(wbuf.at[y_left], wbuf.at[y_left], w_send.at[0], w_recv.at[0], dev_yl).wait_recv()
    w_f = remote(
        wbuf.at[y_left, 0:half], wbuf.at[y_left, 0:half], w_send.at[2], w_recv.at[2], dev_yr
    )
    w_f.start()
    remote(wbuf.at[y_right], wbuf.at[y_right], w_send.at[1], w_recv.at[1], dev_yr).wait_recv()
    w_b = remote(
        wbuf.at[y_right, half : 2 * half], wbuf.at[y_right, half : 2 * half],
        w_send.at[3], w_recv.at[3], dev_yl,
    )
    w_b.start()

    def wait_b(o, _):
        src = lax.rem(s + o, NS)
        remote(pbuf.at[src], pbuf.at[src], b_send.at[o], b_recv.at[src], (src, e)).wait_recv()
        return 0

    lax.fori_loop(1, NS, wait_b, 0)
    for d in range(NS):
        piece = pbuf[d].astype(f32)
        for r in range(4):
            inc[pl.ds(4 * d + r, HEADS, stride=HD), :] = piece[8 * r : 8 * r + 8]
    for h in range(HEADS):
        cols = slice(h * HD, (h + 1) * HD)
        out = loc[:, cols] + jnp.dot(
            qd[:, cols], inc[cols, :].astype(bf16), preferred_element_type=f32
        )
        mean = jnp.mean(out * out, axis=1, keepdims=True)
        gate = 1.0 / (1.0 + jnp.exp(-g_ref[:, cols].astype(f32)))
        act[z, :, cols] = (out * lax.rsqrt(mean + epsilon) * gain_ref[0:1, cols] * gate).astype(
            bf16
        )

    z_right, z_left = lax.rem(z + 1, NZ), lax.rem(z + NZ - 1, NZ)
    dev_zr, dev_zl = (z_right * NY + y, e), (z_left * NY + y, e)

    def at(k):
        return lax.rem(z + k + NZ, NZ)

    def ring(k):
        own_r, own_l = at(1 - k), at(k - 1)
        if k < 4:
            src_r, src_l = act.at[own_r], act.at[own_l]
        else:
            src_r, src_l = act.at[own_r, 0:64], act.at[own_l, 64:128]
        right = remote(src_r, src_r, r_send.at[2 * k - 2], r_recv.at[2 * k - 2], dev_zr)
        left = remote(src_l, src_l, r_send.at[2 * k - 1], r_recv.at[2 * k - 1], dev_zl)
        right.start()
        left.start()
        return right, left

    def ring_wait(k):
        got_r, got_l = at(-k), at(k)
        if k < 4:
            dst_r, dst_l = act.at[got_r], act.at[got_l]
        else:
            dst_r, dst_l = act.at[got_r, 0:64], act.at[got_l, 64:128]
        remote(dst_r, dst_r, r_send.at[2 * k - 2], r_recv.at[2 * k - 2], dev_zl).wait_recv()
        remote(dst_l, dst_l, r_send.at[2 * k - 1], r_recv.at[2 * k - 1], dev_zr).wait_recv()

    sibling = (s, e + 1 - 2 * c)
    mine = pl.ds(pl.multiple_of(c * 64, 64), 64)
    other = pl.ds(pl.multiple_of((1 - c) * 64, 64), 64)

    def product(k):
        blk = at(k)
        pb[blk] = jnp.dot(act[blk], wcat[...], preferred_element_type=f32).astype(bf16)
        remote(
            pb.at[blk, other], sb.at[blk], sb_send.at[blk], sb_recv.at[blk], sibling
        ).start()

    def pass_on(k):
        blk = at(k)
        remote(
            pb.at[blk, other], sb.at[blk], sb_send.at[blk], sb_recv.at[blk], sibling
        ).wait_recv()
        both = (pb[blk, mine].astype(f32) + sb[blk].astype(f32)).astype(bf16)
        qb[blk] = both

        @pl.when(blk != e)
        def _():
            remote(qb.at[blk], rs.at[e], rs_send.at[blk], rs_recv.at[e], (s, blk)).start()

        @pl.when(blk == e)
        def _():
            rs[e] = both

    sends = [ring(1)]
    wl.wait()
    remote(
        wbuf.at[y_far, 0:half], wbuf.at[y_far, 0:half], w_send.at[2], w_recv.at[2], dev_yl
    ).wait_recv()
    remote(
        wbuf.at[y_far, half : 2 * half], wbuf.at[y_far, half : 2 * half],
        w_send.at[3], w_recv.at[3], dev_yr,
    ).wait_recv()
    for part in range(8):
        rows = slice(part * 128, part * 128 + 128)
        acc = jnp.zeros((128, NY * COLS), f32)
        for i in range(NY):
            place = (iota((COLS, NY * COLS), 1) == iota((COLS, NY * COLS), 0) + i * COLS)
            acc += jnp.dot(
                wbuf[i, rows, :], place.astype(f32).astype(bf16), preferred_element_type=f32
            )
        wcat[rows, :] = acc.astype(bf16)
    product(0)
    ring_wait(1)
    sends.append(ring(2))
    product(-1)
    product(1)
    pass_on(0)
    ring_wait(2)
    sends.append(ring(3))
    product(-2)
    product(2)
    pass_on(-1)
    pass_on(1)
    ring_wait(3)
    sends.append(ring(4))
    product(-3)
    product(3)
    pass_on(-2)
    pass_on(2)
    ring_wait(4)
    product(4)
    pass_on(-3)
    pass_on(3)
    pass_on(4)

    def wait_rs(o, _):
        src = lax.rem(e + o, NE)
        remote(rs.at[src], rs.at[src], rs_send.at[src], rs_recv.at[src], (s, src)).wait_recv()
        return 0

    lax.fori_loop(1, NE, wait_rs, 0)
    halves = []
    for core in range(2):
        acc = rs[core].astype(f32)
        for x in range(1, 4):
            acc += rs[2 * x + core].astype(f32)
        halves.append(acc.astype(bf16))
    block = jnp.concatenate(halves, axis=0)
    for i in range(NY):
        take = (iota((NY * COLS, COLS), 0) == iota((NY * COLS, COLS), 1) + i * COLS)
        ysend[i] = jnp.dot(
            block, take.astype(f32).astype(bf16), preferred_element_type=f32
        ).astype(bf16)

    def send_y(o):
        peer = lax.rem(y + o, NY)
        return remote(
            ysend.at[peer], yrecv.at[y], y_send.at[o], y_recv.at[y], (z * NY + peer, e)
        )

    for o in range(1, NY):
        send_y(o).start()
    yrecv[y] = ysend[y]
    for o in range(1, NY):
        src = lax.rem(y + o, NY)
        remote(
            yrecv.at[src], yrecv.at[src], y_send.at[o], y_recv.at[src], (z * NY + src, e)
        ).wait_recv()
    for i in range(NY):
        rows = slice(i * TOK, (i + 1) * TOK)
        after_ref[rows, :] = res_ref[rows, :].astype(f32) + yrecv[i].astype(f32)

    def drain_state(o, _):
        peer = lax.rem(s + o, NS)
        remote(ub.at[peer], rbuf.at[s], a_send.at[o], a_recv.at[s], (peer, e)).wait_send()
        remote(pref.at[peer], pbuf.at[s], b_send.at[o], b_recv.at[s], (peer, e)).wait_send()
        return 0

    lax.fori_loop(1, NS, drain_state, 0)
    for copy in (w_r, w_l, w_f, w_b):
        copy.wait_send()
    for right, left in sends:
        right.wait_send()
        left.wait_send()
    for blk in range(NZ):
        remote(
            pb.at[blk, other], sb.at[blk], sb_send.at[blk], sb_recv.at[blk], sibling
        ).wait_send()

        @pl.when(blk != e)
        def _():
            remote(qb.at[blk], rs.at[e], rs_send.at[blk], rs_recv.at[e], (s, blk)).wait_send()

    for o in range(1, NY):
        send_y(o).wait_send()


def attention(query, key_in, value_in, gate_in, log_decay, state_in, attn_gain, w_out, residual):
    vmem = pl.BlockSpec(memory_space=pltpu.VMEM)
    dma = pltpu.SemaphoreType.DMA
    wide = HEADS * HD
    return pl.pallas_call(
        attention_kernel,
        out_shape=(
            jax.ShapeDtypeStruct((NY * TOK, COLS), f32),
            jax.ShapeDtypeStruct((HEADS, 4, HD), f32),
        ),
        in_specs=[vmem] * 7 + [pl.BlockSpec(memory_space=pl.ANY), vmem],
        out_specs=(vmem, vmem),
        scratch_shapes=[
            pltpu.VMEM((TOK, HD), f32),
            pltpu.VMEM((TOK, HD), f32),
            pltpu.VMEM((HD, TOK), f32),
            pltpu.VMEM((TOK, wide), bf16),
            pltpu.VMEM((wide, HD), f32),
            pltpu.VMEM((NS, 48, HD), bf16),
            pltpu.VMEM((NS, 48, HD), bf16),
            pltpu.VMEM((NS, 32, HD), bf16),
            pltpu.VMEM((NS, 32, HD), bf16),
            pltpu.VMEM((wide, HD), f32),
            pltpu.VMEM((TOK, wide), f32),
            pltpu.VMEM((TOK, wide), bf16),
            pltpu.VMEM((NY, wide, COLS), bf16),
            pltpu.VMEM((wide, NY * COLS), bf16),
            pltpu.VMEM((NZ, TOK, wide), bf16),
            pltpu.VMEM((NZ, TOK, NY * COLS), bf16),
            pltpu.VMEM((NZ, 64, NY * COLS), bf16),
            pltpu.VMEM((NZ, 64, NY * COLS), bf16),
            pltpu.VMEM((NE, 64, NY * COLS), bf16),
            pltpu.VMEM((NY, TOK, COLS), bf16),
            pltpu.VMEM((NY, TOK, COLS), bf16),
            dma(()), dma((4,)), dma((4,)), dma((NS,)), dma((NS,)), dma((NS,)), dma((NS,)),
            dma((8,)), dma((8,)), dma((8,)), dma((8,)), dma((8,)), dma((8,)), dma((4,)), dma((4,)),
        ],
        compiler_params=pltpu.CompilerParams(
            collective_id=0, has_side_effects=True, vmem_limit_bytes=48 * 1024 * 1024
        ),
        name="attention",
    )(
        query, key_in, value_in, gate_in, log_decay, state_in.reshape(wide, HD),
        attn_gain.reshape(1, wide), w_out, residual,
    )


def entering_2(part, axis, combine, identity):
    place = lax.axis_index(axis)
    gathered = lax.all_gather(part, axis)
    state = jnp.zeros_like(part) + jnp.asarray(identity, part.dtype)

    def one(lap, state):
        return combine(state, lax.dynamic_index_in_dim(gathered, lap, 0, False))

    return lax.fori_loop(0, place, one, state)


def add_counts(earlier, later_counts):
    return earlier + later_counts


def local(
    residual,
    query,
    key_in,
    value_in,
    gate_in,
    log_decay,
    state_in,
    attn_gain,
    w_out,
    moe_gain,
    router,
    w_gate,
    w_up,
    w_down,
    expert_ids,
    keep_counts,
):
    after_attn, final_rows = attention(
        query, key_in, value_in, gate_in, log_decay, state_in, attn_gain, w_out, residual
    )
    block_rows = residual.shape[0]
    experts_all = router.shape[1]
    logit_part = jnp.dot(after_attn * moe_gain, router, precision=highest)
    choose = (
        expert_ids[:, :, None] == jnp.arange(experts_all, dtype=jnp.int32)[None, None, :]
    ).astype(jnp.float32)
    chosen_part = jnp.einsum("tke,te->tk", choose, logit_part, precision=highest)
    squares, chosen = lax.psum((jnp.sum(after_attn * after_attn, axis=1), chosen_part), "seq")
    inv_rms = lax.rsqrt(squares / D + epsilon)
    chosen = chosen * inv_rms[:, None]
    gate_probs = jnp.stack(
        [jax.nn.sigmoid(chosen[:, 0] - chosen[:, 1]), jax.nn.sigmoid(chosen[:, 1] - chosen[:, 0])],
        axis=1,
    )
    routed_in = (after_attn * inv_rms[:, None] * moe_gain).astype(jnp.bfloat16)
    lanes = lax.axis_size("exp")
    window = w_gate.shape[0] * lanes
    capacity = 5 * block_rows * lanes // (2 * lanes * experts_all)
    top_count = expert_ids.shape[1]
    flat_ids = expert_ids.reshape(block_rows * top_count)
    onehot = (flat_ids[:, None] == jnp.arange(window, dtype=jnp.int32)[None, :]).astype(jnp.int32)
    local_rank = jnp.sum((jnp.cumsum(onehot, axis=0) - onehot) * onehot, axis=1)
    before = entering_2(jnp.sum(onehot, axis=0), "exp", add_counts, jnp.zeros((window,), jnp.int32))
    global_rank = local_rank + jnp.sum(before[None, :] * onehot, axis=1)
    limits = jnp.sum(keep_counts[None, :window] * onehot, axis=1)
    is_kept = (flat_ids < window) & (global_rank < limits)
    slot_hot = ((local_rank[:, None] == jnp.arange(capacity)[None, :]) & is_kept[:, None]).astype(
        jnp.int32
    )
    assign_int = onehot[:, :, None] * slot_hot[:, None, :]
    assign_table = assign_int.astype(jnp.bfloat16)
    token_table = jnp.sum(
        assign_int.reshape(block_rows, top_count, window, capacity), axis=1
    ).astype(jnp.bfloat16)
    sending = jnp.einsum(
        "tec,td->ecd", token_table, routed_in, preferred_element_type=jnp.float32
    ).astype(jnp.bfloat16)
    arrived = lax.all_to_all(sending, "exp", split_axis=0, concat_axis=1, tiled=True)
    contract_dims = (((1,), (1,)), ((), ()))
    portion = lax.all_gather(arrived, "seq", axis=2, tiled=True)
    gate_cols = w_gate[0]
    up_cols = w_up[0]
    gate_add = lax.dot_general(
        portion[0], gate_cols, contract_dims, preferred_element_type=jnp.float32
    )
    up_add = lax.dot_general(portion[0], up_cols, contract_dims, preferred_element_type=jnp.float32)
    hidden = (jax.nn.silu(gate_add) * up_add).astype(jnp.bfloat16)
    down_rows = w_down[0]
    result = jnp.dot(
        lax.all_gather(hidden, "seq", axis=1, tiled=True),
        down_rows,
        preferred_element_type=jnp.float32,
    )
    expert_out = result.astype(jnp.bfloat16)[None]
    returned = lax.all_to_all(expert_out, "exp", split_axis=1, concat_axis=0, tiled=True)
    picked = jnp.einsum(
        "aec,ecd->ad", assign_table, returned, preferred_element_type=jnp.float32
    ).reshape(block_rows, top_count, -1)
    weight = jnp.where(is_kept.reshape(block_rows, top_count), gate_probs, 0.0)
    expert_sum = jnp.sum(picked * weight[:, :, None], axis=1)
    return ((after_attn + expert_sum).astype(jnp.bfloat16), final_rows)


def solution(mesh):
    in_specs = (
        P("exp", "seq"),
        P("seq", "exp"),
        P("seq", "exp"),
        P("seq", "exp"),
        P("seq", "exp"),
        P("seq", "exp"),
        P("exp", None, None),
        P("exp"),
        P("exp", "seq"),
        P("seq"),
        P("seq", None),
        P("exp", "seq", None),
        P("exp", "seq", None),
        P("exp", None, "seq"),
        P("exp", None),
        P(),
    )
    out_specs = (P("exp", "seq"), P("exp", "seq", None))
    return jax.shard_map(local, mesh=mesh, in_specs=in_specs, out_specs=out_specs, check_vma=False)
```

time: 774 us -> 471 us (0.61)
  waiting for transfers between devices: 502 us -> 174 us
  Pallas kernels: 0 us -> 68 us
  blocking collectives: 131 us -> 103 us
  matrix products: 34.9 us -> 18.8 us
  local copies, waits for them, and re-layouts: 38 us -> 51.1 us
    all_gather x2 -> x0, waiting for transfers between devices: 215 us -> none  [the longest x1 157 us: local(): gathered = lax.all_gather(heads_mixed, 'seq', axis=0, tiled=True)]
    psum x1 -> x0, waiting for transfers between devices: 123 us -> none  [broadcast(): return lax.psum(kept, axis)]
    pallas_call x0 -> x1, Pallas kernels: none -> 68 us  [attention(): pl.pallas_call(attention_kernel, out_shape=(jax.ShapeDtypeStruct((NY * TO...]
    all_gather x1 -> x0, blocking collectives: 36.3 us -> none  [entering(): lax.all_gather(a.astype(kind), axis)]
    unnamed x1, blocking collectives: 8.96 us -> 25.2 us
    dot_general x5 -> x0, matrix products: 16.2 us -> none  [the longest x1 7.51 us: local(): jnp.dot(gathered, w_out, preferred_element_type=jnp.float32)]
    unnamed x30 -> x45, local copies, waits for them, and re-layouts: 11.4 us -> 27.3 us
    all_to_all x1, blocking collectives: 27.6 us -> 18.8 us  [local(): lax.all_to_all(sending, 'exp', split_axis=0, concat_axis=1, tiled=True)]
  transfers between devices with their start and end apart: 7 -> 3, of which waited for: 5 -> 3; matrix products, arithmetic and copies ran while one was open for 7% -> 0% of each run, Pallas kernels for 0% -> 0%
where the time goes in v1:
time: 471 us; the launch traced here: 468 us
  waiting for transfers between devices  174 us (37%)
  blocking collectives  103 us (22%)
  Pallas kernels  68 us (14%)
  local copies, waits for them, and re-layouts  51.1 us (11%)
  other arithmetic  33.5 us (7%)
  matrix products  18.8 us (4%)
  between operations  14.8 us (3%)
  starting transfers between devices  5.49 us (1%)
    all_gather x1, waiting for transfers between devices, local(): lax.all_gather(hidden, 'seq', axis=1, tiled=True)  92.3 us
    all_gather x1, waiting for transfers between devices, local(): portion = lax.all_gather(arrived, 'seq', axis=2, tiled=True)  76.6 us
    pallas_call x1, Pallas kernels, attention(): pl.pallas_call(attention_kernel, out_shape=(jax.ShapeDtypeStruct((NY * TO...  68 us
    psum x1, blocking collectives, local(): lax.psum((jnp.sum(after_attn * after_attn, axis=1), chosen_part), 'seq')  58.7 us
    unnamed x45, local copies, waits for them, and re-layouts  27.3 us
    unnamed x1, blocking collectives  25.2 us
    all_to_all x1, blocking collectives, local(): lax.all_to_all(sending, 'exp', split_axis=0, concat_axis=1, tiled=True)  18.8 us
    unnamed x3, other arithmetic  12.7 us
  transfers between devices with their start and end apart: 3, of which 3 were waited for; matrix products, arithmetic and copies ran while one was open for 0% of the time, Pallas kernels for 0%

profile of v1, /device:TPU:1, one launch (start us, length us, event | category | flops | bytes accessed | tf_op | source)
XLA Modules:
  0.0 468.5 jit_solution(5458435376685008061)
XLA Ops:
  8.9 1.7 eq.78
  13.6 2.0 copy.80.w_hbm
  15.6 1.8 copy.81.res_ref
  27.2 68.0 %attention.1 = (f32[512,192]{1,0:T(8,128)S(1)}, f32[8,4,128]{2,1,0:T(4,128)S(1)}) custom-call(bf16[128,1024]{1,0:T(8,128)(2,1)S(1)} %copy-done.5, bf16[128,1024]{1,0:T(8,128)(2,1)S(1)} %copy-done.6, bf16[128,1024]{1,0:T(8,128)(2,1)S(1)} %copy-done.7, bf16[128,1024]{1,0:T(8,128)(2,1)S(1)} %copy-done.8, f32[128,8]{1,0:T(8,128)S(1)} %copy-done.9, ...), custom_call_target="tpu_custom_call" | custom-call | tf_op jit(solution)/shard_map/attention/pallas_call | solution.py:345
  97.3 8.0 %fusion.28 = f32[512,2]{1,0:T(8,128)} fusion(f32[512,32]{1,0:T(8,128)S(1)} %fusion.29, s32[512,2]{1,0:T(8,128)S(1)} %copy-done.11), kind=kLoop, calls=%fused_computation.22 | loop fusion | flops 97280 | bytes 73728
  107.0 58.7 %all-reduce.1 = (f32[512]{0:T(512)}, f32[512,2]{0,1:T(2,128)}) all-reduce(f32[512]{0:T(512)} %multiply_reduce_fusion.1, f32[512,2]{0,1:T(2,128)} %copy.100), channel_id=1, replica_groups=mesh['seq'=32,'exp'=8] {'seq'}, use_global_device_ids=true, to_apply=%region_10.11 | all-reduce | flops 1536 | bytes 12288 | tf_op jit(solution)/shard_map/psum | solution.py:431
  169.6 5.1 %reduce-window.6 = s32[8,8,128]{2,1,0:T(8,128)} reduce-window(s32[8,8,128]{2,1,0:T(8,128)} %fusion.42, s32[]{:T(128)} %constant.17.clone.1), window={size=1x1x128 pad=0_0x0_0x127_0}, to_apply=%region_0.0 | reduce-window | flops 1040384 | bytes 65540 | tf_op jit(solution)/shard_map/reduce-window
  184.3 25.2 %all-reduce = s32[64]{0:T(128)} all-reduce(s32[64]{0:T(128)} %dynamic-update-slice), channel_id=2, replica_groups=mesh['seq'=32,'exp'=8] {'exp'}, use_global_device_ids=true, to_apply=%add | all-reduce | flops 64 | bytes 512
  228.2 18.8 %all_to_all.24 = bf16[8,40,192]{2,1,0:T(8,128)(2,1)} all-to-all(bf16[8,40,192]{2,1,0:T(8,128)(2,1)S(1)} %convolution_convert_fusion), channel_id=1, replica_groups=mesh['seq'=32,'exp'=8] {'exp'}, dimensions={0} | all-to-all | bytes 245760 | tf_op jit(solution)/shard_map/all_to_all | solution.py:461
  248.8 76.6 %all-gather.4.cloned.1.call-done = bf16[1,320,6144]{1,2,0:T(8,128)(2,1)} async-done(((bf16[1,320,192]{1,2,0:T(8,128)(2,1)}), bf16[1,320,6144]{1,2,0:T(8,128)(2,1)}) %all-gather.4.cloned.1.call-update) | async-done | bytes 3932176 | tf_op jit(solution)/shard_map/all_gather | solution.py:463
  325.3 4.5 fusion
  330.2 2.7 fusion.15
  332.9 92.3 %all-gather.6.cloned.1.call-done = bf16[320,9216]{0,1:T(8,128)(2,1)} async-done(((bf16[320,288]{0,1:T(8,128)(2,1)}), bf16[320,9216]{0,1:T(8,128)(2,1)}) %all-gather.6.cloned.1.call-update) | async-done | bytes 5898256 | tf_op jit(solution)/shard_map/all_gather | solution.py:473
  425.2 6.8 %fusion.23 = bf16[1,320,192]{1,2,0:T(8,128)(2,1)} fusion(bf16[320,9216]{0,1:T(8,128)(2,1)} %all-gather.6.cloned.1.call-done, bf16[1,9216,192]{1,2,0:T(8,128)(2,1)} %param.31), kind=kOutput, calls=%fused_computation.18 | convolution fusion | flops 1132523520 | bytes 9560064 | tf_op jit(solution)/shard_map/dot_general | solution.py:472
  431.9 1.8 copy.90
  434.3 3.2 reduce.4
  437.5 1.8 reshape.170
  439.3 5.4 %all-to-all-start.1 = ((bf16[8,2,3840]{2,1,0:T(2,128)(2,1)}), bf16[8,2,3840]{2,1,0:T(2,128)(2,1)}, u32[]{:S(2)}, u32[]{:S(2)}) async-start(bf16[8,2,3840]{2,1,0:T(2,128)(2,1)} %reshape.170), calls=%async_computation.1 | async-start | bytes 245760 | tf_op jit(solution)/shard_map/all_to_all | solution.py:478
  444.7 5.3 %all-to-all-done.1 = bf16[8,2,3840]{2,1,0:T(2,128)(2,1)} async-done(((bf16[8,2,3840]{2,1,0:T(2,128)(2,1)}), bf16[8,2,3840]{2,1,0:T(2,128)(2,1)}, u32[]{:S(2)}, u32[]{:S(2)}) %all-to-all-start.1) | async-done | bytes 122912 | tf_op jit(solution)/shard_map/all_to_all | solution.py:478
  449.9 2.3 reshape.171
  453.2 2.1 fusion.9
  455.3 2.0 copy.92
  457.3 2.0 add_convert_fusion
  459.3 1.8 copy.93
  (73 shorter events, 55.4 us)
Async XLA Ops:
  7.2 318.2 %copy-start = (bf16[1,288,6144]{2,1,0:T(8,128)(2,1)S(1)}, bf16[1,288,6144]{2,1,0:T(8,128)(2,1)}, u32[]{:S(2)}) copy-start(bf16[1,288,6144]{2,1,0:T(8,128)(2,1)} %param.29) | copy-start | bytes 10616836
  7.2 318.2 %all-gather.4.cloned.1.call-start = ((), (), s32[]{:S(2)}) async-start(), calls=%async_computation.2 | async-start | bytes 4866048 | tf_op jit(solution)/shard_map/all_gather | solution.py:463
  18.8 1.0 copy-start.2
  19.8 0.9 copy-start.3
  20.8 1.0 copy-start.4
  21.8 0.9 copy-start.5
  22.8 0.9 copy-start.6
  23.7 0.9 copy-start.7
  24.7 0.9 copy-start.8
  25.6 0.8 copy-start.9
  26.5 0.7 copy-start.10
  27.2 70.2 %copy-start.11 = (s32[512,2]{1,0:T(8,128)S(1)}, s32[512,2]{1,0:T(8,128)}, u32[]{:S(2)}) copy-start(s32[512,2]{1,0:T(8,128)} %copy.82) | copy-start | bytes 12292
  95.2 0.8 copy-start.1
  166.4 0.6 copy-start.13
  225.9 21.1 %copy-start.12 = (s32[512,2,40]{0,2,1:T(8,128)}, s32[512,2,40]{0,2,1:T(8,128)S(1)}, u32[]{:S(2)}) copy-start(s32[512,2,40]{0,2,1:T(8,128)S(1)} %fusion.38) | copy-start | bytes 491524
  248.7 176.4 %all-gather.6.cloned.1.call-start = ((), (), s32[]{:S(2)}) async-start(), calls=%async_computation.3 | async-start | bytes 7299072 | tf_op jit(solution)/shard_map/all_gather | solution.py:473
  325.3 4.5 copy-start.14
  325.3 4.9 %copy-start.15 = (bf16[1,288,6144]{2,1,0:T(8,128)(2,1)S(1)}, bf16[1,288,6144]{2,1,0:T(8,128)(2,1)}, u32[]{:S(2)}) copy-start(bf16[1,288,6144]{2,1,0:T(8,128)(2,1)} %param.30) | copy-start | bytes 10616836
  439.3 10.7 %all-to-all-start.1 = ((bf16[8,2,3840]{2,1,0:T(2,128)(2,1)}), bf16[8,2,3840]{2,1,0:T(2,128)(2,1)}, u32[]{:S(2)}, u32[]{:S(2)}) async-start(bf16[8,2,3840]{2,1,0:T(2,128)(2,1)} %reshape.170), calls=%async_computation.1 | async-start | bytes 245760 | tf_op jit(solution)/shard_map/all_to_all | solution.py:478
Sparse Core Ops, SparseCore 0:
  248.9 76.4 all-gather.3
  333.0 92.1 all-gather.5

commit v2 on v1

v2 whole, which is shorter than its diff:
```python
import jax
import jax.numpy as jnp
from jax import lax
from jax.experimental import pallas as pl
from jax.experimental.pallas import tpu as pltpu
from jax.sharding import PartitionSpec as P

f32, bf16 = jnp.float32, jnp.bfloat16
highest = lax.Precision.HIGHEST
epsilon = 1e-05
D = 6144
NS, NE, NY, NZ = 32, 8, 4, 8
HEADS, HD, TOK = 8, 128, 128
COLS = 192
MESH = pl.DeviceIdType.MESH


def silu(v):
    return v / (1.0 + jnp.exp(-v))


def iota(shape, dim):
    return lax.broadcasted_iota(jnp.int32, shape, dim)


def remote(src, dst, send, recv, dev):
    return pltpu.make_async_remote_copy(
        src_ref=src, dst_ref=dst, send_sem=send, recv_sem=recv, device_id=dev, device_id_type=MESH
    )


def enter(s, e):
    barrier = pltpu.get_barrier_semaphore()

    def seq_signal(o, _):
        pl.semaphore_signal(
            barrier, inc=1, device_id=(lax.rem(s + o, NS), e), device_id_type=MESH
        )
        return 0

    def exp_signal(o, _):
        pl.semaphore_signal(
            barrier, inc=1, device_id=(s, lax.rem(e + o, NE)), device_id_type=MESH
        )
        return 0

    lax.fori_loop(1, NS, seq_signal, 0)
    lax.fori_loop(1, NE, exp_signal, 0)
    return barrier


def layer_kernel(
    q_ref, k_ref, v_ref, g_ref, ld_ref, st_ref, gain_ref, w_hbm, res_ref,
    mgain_ref, router_ref, ids_ref, keep_ref, wg_hbm, wu_hbm, wd_hbm,
    out_ref, fin_ref,
    ldp, lcol, lrow, kbf, upd, ub, rbuf, pref, pbuf, inc, loc, qd,
    wcat, act, pb, sb, qb, rs, ysend, yrecv,
    after, slot_mask, combine, place, cnt, stat, inv_send, inv_recv,
    disp, disp_in, back, back_in, x_a, x_b, x_r, h_a, h_b, h_r, wg, wu, wd, acc_g, acc_u,
    w_local, w_send, w_recv, a_send, a_recv, b_send, b_recv,
    r_send, r_recv, sb_send, sb_recv, rs_send, rs_recv, y_send, y_recv,
    big, c_send, c_recv, t_send, t_recv, i_send, i_recv, d_send, d_recv, o_send, o_recv,
    ag_send, ag_recv,
):
    s = lax.axis_index("seq")
    e = lax.axis_index("exp")
    y, z = lax.rem(s, NY), s // NY
    c = lax.rem(e, 2)
    barrier = enter(s, e)

    def cols_of(at, first, count):
        return pl.ds(pl.multiple_of(at * COLS + first, 16), count)

    wl = pltpu.make_async_copy(w_hbm, wcat.at[cols_of(y, 0, COLS)], w_local)
    wl.start()
    loads = [
        pltpu.make_async_copy(src, dst, big.at[i])
        for i, (src, dst) in enumerate(((wg_hbm, wg), (wu_hbm, wu), (wd_hbm, wd)))
    ]
    for load in loads:
        load.start()

    ids = [ids_ref[k : k + 1, :] for k in range(2)]
    hot = [(iota((8, 512), 0) == ids[k]).astype(f32) for k in range(2)]
    held = hot[0] + hot[1]

    def exp_copy(src, dst, send, recv, o):
        peer = lax.rem(e + o, NE)
        return remote(src(peer), dst.at[e], send.at[o], recv.at[e], (s, peer))

    def exp_wait(dst, send, recv):
        def one(o, _):
            src = lax.rem(e + o, NE)
            remote(dst.at[src], dst.at[src], send.at[o], recv.at[src], (s, src)).wait_recv()
            return 0

        lax.fori_loop(1, NE, one, 0)

    def exp_start(src, dst, send, recv):
        def one(o, _):
            exp_copy(src, dst, send, recv, o).start()
            return 0

        lax.fori_loop(1, NE, one, 0)

    def count_tokens():
        totals = jnp.sum(held, axis=1, keepdims=True)
        cnt[e] = jnp.broadcast_to(totals, (8, 128))
        exp_start(lambda peer: cnt.at[e], cnt, c_send, c_recv)

    def ranks():
        later = (iota((512, 512), 0) < iota((512, 512), 1)).astype(f32).astype(bf16)
        return jnp.dot(held.astype(bf16), later, preferred_element_type=f32)

    def slots(earlier):
        found = []
        for k in range(2):
            rank = jnp.sum(hot[k] * earlier, axis=0, keepdims=True).astype(jnp.int32)
            found.append(jnp.where(ids[k] < 8, ids[k] * 128 + rank, -1))
        return found

    def prepare():
        for g in range(3):
            for b in range(NE):
                lane = iota((128, 384), 0) - 40 * g
                hit = (iota((128, 384), 1) == lane + 40 * b) & (lane >= 0) & (lane < 40)
                place[g, b * 128 : b * 128 + 128, :] = jnp.where(hit, 1.0, 0.0).astype(bf16)
        slot = slots(ranks())
        for b in range(NE):
            at_row = iota((128, 512), 0) + b * 128
            hit = (at_row == slot[0]) | (at_row == slot[1])
            slot_mask[b * 128 : b * 128 + 128, :] = jnp.where(hit, 1.0, 0.0).astype(bf16)

    def by_lanes(a, b):
        return lax.dot_general(a, b, (((1,), (1,)), ((), ())), preferred_element_type=f32)

    def split(row):
        one = row.astype(bf16).astype(f32)
        two = (row - one).astype(bf16).astype(f32)
        return jnp.concatenate([one, two, row - one - two] + [jnp.zeros_like(row)] * 5, axis=0)

    def gather(a, b, turn, cut, hook):
        z_r, z_l = lax.rem(z + 1, NZ) * NY + y, lax.rem(z + NZ - 1, NZ) * NY + y
        y_r, y_l = z * NY + lax.rem(y + 1, NY), z * NY + lax.rem(y + NY - 1, NY)
        dev_z, dev_y = ((z_r, e), (z_l, e)), ((y_r, e), (y_l, e))
        rows_a, rows_b = a.shape[2], b.shape[2]
        started = []

        def zz(k):
            return lax.rem(z + k + NZ, NZ)

        def yy(k):
            return lax.rem(y + k + NY, NY)

        def move(ref, index, dev):
            return remote(ref, ref, ag_send.at[turn, index], ag_recv.at[turn, index], dev)

        def go(ref, index, dev):
            started.append(move(ref, index, dev))
            started[-1].start()

        def come(ref, index, dev):
            move(ref, index, dev).wait_recv()

        def a_y(step, way):
            k = (1 - step if way == 0 else step - 1) if step > 0 else 0
            return k

        def a1(step, do, take):
            for way in range(2):
                sign = -1 if way == 0 else 1
                k = sign * (step if take else step - 1)
                ref = a.at[z, yy(k)]
                if step == 2:
                    ref = a.at[z, yy(k), way * (rows_a // 2) : (way + 1) * (rows_a // 2)]
                do(ref, 2 * step - 2 + way, dev_y[1 - way if take else way])

        def a2(step, do, take):
            for way in range(2):
                sign = -1 if way == 0 else 1
                k = sign * (step if take else step - 1)
                ref = a.at[zz(k)]
                if step == 4:
                    ref = a.at[zz(k), 2 * way : 2 * way + 2]
                do(ref, 4 + 2 * step - 2 + way, dev_z[1 - way if take else way])

        def b1(step, do, take):
            for way in range(2):
                sign = -1 if way == 0 else 1
                k = sign * (step if take else step - 1)
                ref = b.at[zz(k), y]
                if step == 4:
                    ref = b.at[zz(k), y, 0:cut] if way == 0 else b.at[zz(k), y, cut:rows_b]
                do(ref, 12 + 2 * step - 2 + way, dev_z[1 - way if take else way])

        def b2(step, at_z, do, take):
            for way in range(2):
                sign = -1 if way == 0 else 1
                k = sign * (step if take else step - 1)
                ref = b.at[zz(at_z), yy(k)]
                if step == 2:
                    ref = (
                        b.at[zz(at_z), yy(k), 0:cut]
                        if way == 0
                        else b.at[zz(at_z), yy(k), cut:rows_b]
                    )
                index = 20 + 4 * (at_z + 3) + 2 * step - 2 + way
                do(ref, index, dev_y[1 - way if take else way])

        def turn_b(*ks):
            for k in ks:
                b2(1, k, come, True)
                b2(2, k, go, False)

        a1(1, go, False)
        b1(1, go, False)
        b2(1, 0, go, False)
        a1(1, come, True)
        a1(2, go, False)
        hook()
        b1(1, come, True)
        b1(2, go, False)
        b2(1, -1, go, False)
        b2(1, 1, go, False)
        a1(2, come, True)
        a2(1, go, False)
        turn_b(0)
        b1(2, come, True)
        b1(3, go, False)
        b2(1, -2, go, False)
        b2(1, 2, go, False)
        turn_b(-1, 1)
        b1(3, come, True)
        b1(4, go, False)
        b2(1, -3, go, False)
        b2(1, 3, go, False)
        a2(1, come, True)
        a2(2, go, False)
        b1(4, come, True)
        b2(1, 4, go, False)
        turn_b(-2, 2)
        a2(2, come, True)
        a2(3, go, False)
        turn_b(-3, 3)
        a2(3, come, True)
        a2(4, go, False)
        turn_b(4)
        a2(4, come, True)
        for k in range(-3, 5):
            b2(2, k, come, True)
        return started

    def unpack(src, first, rows, dst):
        swap = (iota((128, 128), 0) == lax.rem(iota((128, 128), 1) + 64, 128)).astype(f32)
        swap = swap.astype(bf16)

        def one(i, _):
            zi, yi = i // NY, lax.rem(i, NY)
            part = src[zi, yi, first : first + rows, :]
            dst[zi, yi, 0:rows, :] = part
            dst[zi, yi, rows : 2 * rows, :] = jnp.dot(
                part, swap, preferred_element_type=f32
            ).astype(bf16)
            return 0

        lax.fori_loop(0, NS, one, 0)

    def own_pieces(full, a, b):
        rows = a.shape[2]
        a[z, y] = full[:, 0:128].astype(bf16)
        b[z, y, 0:rows, :] = full[:, 128:256].astype(bf16)
        rest = jnp.where(iota((rows, 128), 1) < 64, full[:, 256:384], 0.0)
        packed = rest[0 : rows // 2] + pltpu.roll(rest[rows // 2 : rows], 64, 1)
        b[z, y, rows : rows + rows // 2, :] = packed.astype(bf16)

    drains = []

    def experts():
        eye = iota((COLS, COLS), 0) == iota((COLS, COLS), 1)
        gain_col = jnp.sum(jnp.where(eye, mgain_ref[...], 0.0), axis=1, keepdims=True)
        rows = after[...]
        squares = jnp.sum(rows * rows, axis=0, keepdims=True)
        logits = jnp.dot(
            router_ref[...] * mgain_ref[...], rows, preferred_element_type=f32, precision=highest
        )
        lane_e = iota((32, 512), 0)
        signed = (lane_e == ids[0]).astype(f32) - (lane_e == ids[1]).astype(f32)
        diff = jnp.sum(signed * logits, axis=0, keepdims=True)
        parts = [r[:, i * 128 : i * 128 + 128] for r in (squares, diff) for i in range(4)]
        stat[s] = jnp.concatenate(parts, axis=0)

        def send_t(o, _):
            peer = lax.rem(s + o, NS)
            remote(stat.at[s], stat.at[s], t_send.at[o], t_recv.at[s], (peer, e)).start()
            return 0

        scaled = (rows * gain_col).astype(bf16)
        packed = [jnp.zeros((64, 128), f32) for _ in range(NE)]
        for g in range(3):
            chosen = by_lanes(scaled[64 * g : 64 * g + 64, :], slot_mask[...])
            for b in range(NE):
                tile = chosen[:, b * 128 : b * 128 + 128]
                packed[b] = packed[b] + (pltpu.roll(tile, 40 * g, 1) if g else tile)
        for b in range(NE):
            disp[b] = packed[b].astype(bf16)
        exp_start(lambda peer: disp.at[peer], disp_in, d_send, d_recv)
        lax.fori_loop(1, NS, send_t, 0)
        disp_in[e] = disp[e]
        exp_wait(disp_in, d_send, d_recv)
        arrived = jnp.concatenate([disp_in[b] for b in range(NE)], axis=1)
        full = jnp.concatenate(
            [jnp.dot(arrived, place[g], preferred_element_type=f32) for g in range(3)], axis=0
        )
        own_pieces(full, x_a, x_b)

        def weights():
            def wait_t(o, _):
                src = lax.rem(s + o, NS)
                remote(
                    stat.at[src], stat.at[src], t_send.at[o], t_recv.at[src], (src, e)
                ).wait_recv()
                return 0

            lax.fori_loop(1, NS, wait_t, 0)
            total = lax.fori_loop(0, NS, lambda j, t: t + stat[j], jnp.zeros((8, 128), f32))
            sq = jnp.concatenate([total[i : i + 1] for i in range(4)], axis=1)
            gap = jnp.concatenate([total[i : i + 1] for i in range(4, 8)], axis=1)
            inv = lax.rsqrt(sq / D + epsilon)
            gap = gap * inv
            per_slot = by_lanes(split(inv).astype(bf16), slot_mask[...])
            per_slot = per_slot[0:1] + per_slot[1:2] + per_slot[2:3]
            for b in range(NE):
                inv_send[b] = jnp.broadcast_to(per_slot[:, b * 128 : b * 128 + 128], (8, 128))
            exp_start(lambda peer: inv_send.at[peer], inv_recv, i_send, i_recv)
            inv_recv[e] = inv_send[e]
            exp_wait(cnt, c_send, c_recv)
            before = lax.fori_loop(
                0, NE, lambda j, t: t + jnp.where(j < e, cnt[j], 0.0), jnp.zeros((8, 128), f32)
            )
            keep = jnp.where(iota((8, 32), 0) == iota((8, 32), 1), keep_ref[...], 0).astype(f32)
            limit = jnp.sum(keep, axis=1, keepdims=True) - before[:, 0:1]
            earlier = ranks()
            fits = (earlier < limit).astype(f32)
            slot = slots(earlier)
            prob = [1.0 / (1.0 + jnp.exp(-gap)), 1.0 / (1.0 + jnp.exp(gap))]
            weight = [jnp.sum(hot[k] * fits, axis=0, keepdims=True) * prob[k] for k in range(2)]
            for b in range(NE):
                at_row = iota((128, 512), 0) + b * 128
                value = jnp.where(at_row == slot[0], weight[0], 0.0)
                value = jnp.where(at_row == slot[1], weight[1], value)
                combine[b * 128 : b * 128 + 128, :] = value.astype(bf16)

        drains.extend(gather(x_a, x_b, 0, 144, weights))
        unpack(x_b, 192, 96, x_r)
        exp_wait(inv_recv, i_send, i_recv)
        row = jnp.concatenate([inv_recv[b][0:1] for b in range(NE)], axis=1)
        inv_row = jnp.dot(split(row).astype(bf16), place[0], preferred_element_type=f32)
        inv_row = inv_row[0:1] + inv_row[1:2] + inv_row[2:3]
        loads[0].wait()
        loads[1].wait()
        for zi in range(NZ):
            k = slice(zi * 768, zi * 768 + 768)
            piece = jnp.concatenate(
                [
                    x_a[zi].reshape(768, 128),
                    x_b[zi, :, 0:192, :].reshape(768, 128),
                    x_r[zi].reshape(768, 128),
                ],
                axis=1,
            )
            for weight, acc in ((wg, acc_g), (wu, acc_u)):
                part = jnp.dot(weight[:, k], piece, preferred_element_type=f32)
                acc[...] = part if zi == 0 else acc[...] + part
        gate = acc_g[...] * inv_row
        own_pieces(silu(gate) * (acc_u[...] * inv_row), h_a, h_b)
        drains.extend(gather(h_a, h_b, 1, 224, lambda: None))
        unpack(h_b, 288, 144, h_r)
        loads[2].wait()
        total = jnp.zeros((COLS, 384), f32)
        for zi in range(NZ):
            k = slice(zi * 1152, zi * 1152 + 1152)
            piece = jnp.concatenate(
                [
                    h_a[zi].reshape(1152, 128),
                    h_b[zi, :, 0:288, :].reshape(1152, 128),
                    h_r[zi].reshape(1152, 128),
                ],
                axis=1,
            )
            total = total + jnp.dot(wd[:, k], piece, preferred_element_type=f32)
        result = total.astype(bf16)
        packed = by_lanes(result[0:64], place[0])
        for g in range(1, 3):
            packed = packed + by_lanes(result[64 * g : 64 * g + 64], place[g])
        for b in range(NE):
            back[b] = packed[:, b * 128 : b * 128 + 128].astype(bf16)
        exp_start(lambda peer: back.at[peer], back_in, o_send, o_recv)
        back_in[e] = back[e]
        exp_wait(back_in, o_send, o_recv)
        tiles = [back_in[b].astype(f32) for b in range(NE)]
        for g in range(3):
            moved = [pltpu.roll(t, 128 - 40 * g, 1) if g else t for t in tiles]
            picked = jnp.dot(
                jnp.concatenate(moved, axis=1).astype(bf16), combine[...],
                preferred_element_type=f32,
            )
            r = slice(64 * g, 64 * g + 64)
            out_ref[r, :] = (after[r, :] + picked).astype(bf16)

    def drain_experts():
        for copy in drains:
            copy.wait_send()

        def one(o, _):
            exp_copy(lambda peer: cnt.at[e], cnt, c_send, c_recv, o).wait_send()
            exp_copy(lambda peer: disp.at[peer], disp_in, d_send, d_recv, o).wait_send()
            exp_copy(lambda peer: inv_send.at[peer], inv_recv, i_send, i_recv, o).wait_send()
            exp_copy(lambda peer: back.at[peer], back_in, o_send, o_recv, o).wait_send()
            return 0

        def stats(o, _):
            peer = lax.rem(s + o, NS)
            remote(stat.at[s], stat.at[s], t_send.at[o], t_recv.at[s], (peer, e)).wait_send()
            return 0

        lax.fori_loop(1, NE, one, 0)
        lax.fori_loop(1, NS, stats, 0)

    ldp[...] = jnp.zeros_like(ldp)
    ldp[0:HEADS, :] = ld_ref[...]
    tri = (iota((TOK, TOK), 0) <= iota((TOK, TOK), 1)).astype(f32)
    run = jnp.dot(ldp[...], tri, preferred_element_type=f32, precision=highest)
    lrow[...] = run
    lcol[...] = run.T
    for h in range(HEADS):
        cols = slice(h * HD, (h + 1) * HD)
        kh = silu(k_ref[:, cols].astype(f32))
        kbf[:, cols] = kh.astype(bf16)
        tail = jnp.exp(lcol[TOK - 1 : TOK, h : h + 1] - lcol[:, h : h + 1])
        kd = (kh * tail).T.astype(bf16)
        upd[cols, :] = jnp.dot(kd, v_ref[:, cols], preferred_element_type=f32)
    total = jnp.broadcast_to(lrow[0:HEADS, TOK - 1 : TOK], (HEADS, HD))
    high = total.astype(bf16).astype(f32)
    logs = jnp.concatenate([high, total - high], axis=0).astype(bf16)
    for d in range(NS):
        rows = [upd[pl.ds(4 * d + r, HEADS, stride=HD), :] for r in range(4)]
        ub[d, 0:32, :] = jnp.concatenate(rows, axis=0).astype(bf16)
        ub[d, 32:48, :] = logs

    pl.semaphore_wait(barrier, NS - 1 + NE - 1)

    def send_a(o, _):
        peer = lax.rem(s + o, NS)
        remote(ub.at[peer], rbuf.at[s], a_send.at[o], a_recv.at[s], (peer, e)).start()
        return 0

    lax.fori_loop(1, NS, send_a, 0)
    count_tokens()
    rbuf[s] = ub[s]
    y_right, y_left = lax.rem(y + 1, NY), lax.rem(y + NY - 1, NY)
    y_far = lax.rem(y + 2, NY)
    dev_yr, dev_yl = (z * NY + y_right, e), (z * NY + y_left, e)
    w_r = remote(w_hbm, wcat.at[cols_of(y, 0, COLS)], w_send.at[0], w_recv.at[0], dev_yr)
    w_l = remote(w_hbm, wcat.at[cols_of(y, 0, COLS)], w_send.at[1], w_recv.at[1], dev_yl)
    w_r.start()
    w_l.start()

    causal = iota((TOK, TOK), 0) >= iota((TOK, TOK), 1)
    for h in range(HEADS):
        cols = slice(h * HD, (h + 1) * HD)
        qh = silu(q_ref[:, cols].astype(f32))
        lc = lcol[:, h : h + 1]
        gap = lc - lrow[h : h + 1, :]
        decay = jnp.where(causal, jnp.exp(jnp.where(causal, gap, 0.0)), 0.0)
        scores = lax.dot_general(
            qh.astype(bf16), kbf[:, cols], (((1,), (1,)), ((), ())), preferred_element_type=f32
        )
        loc[:, cols] = jnp.dot(
            (scores * decay).astype(bf16), v_ref[:, cols], preferred_element_type=f32
        )
        qd[:, cols] = (qh * jnp.exp(lc)).astype(bf16)

    def wait_a(o, _):
        src = lax.rem(s + o, NS)
        remote(rbuf.at[src], rbuf.at[src], a_send.at[o], a_recv.at[src], (src, e)).wait_recv()
        return 0

    lax.fori_loop(1, NS, wait_a, 0)
    start = jnp.concatenate(
        [st_ref[pl.ds(4 * s + r, HEADS, stride=HD), :] for r in range(4)], axis=0
    )

    def scan(j, state):
        pref[j] = state.astype(bf16)
        piece = rbuf[j].astype(f32)
        dec = jnp.exp(piece[32:40] + piece[40:48])
        return state * jnp.concatenate([dec] * 4, axis=0) + piece[0:32]

    last = lax.fori_loop(0, NS, scan, start)
    for r in range(4):
        for h in range(HEADS):
            fin_ref[h, r : r + 1, :] = last[8 * r + h : 8 * r + h + 1, :]

    def send_b(o, _):
        peer = lax.rem(s + o, NS)
        remote(pref.at[peer], pbuf.at[s], b_send.at[o], b_recv.at[s], (peer, e)).start()
        return 0

    lax.fori_loop(1, NS, send_b, 0)
    pbuf[s] = pref[s]
    half = COLS // 2

    def w_half(at, part):
        return wcat.at[cols_of(at, part * half, half)]

    w_whole = [wcat.at[cols_of(at, 0, COLS)] for at in (y_left, y_right)]
    remote(w_whole[0], w_whole[0], w_send.at[0], w_recv.at[0], dev_yl).wait_recv()
    w_f = remote(w_half(y_left, 0), w_half(y_left, 0), w_send.at[2], w_recv.at[2], dev_yr)
    w_f.start()
    remote(w_whole[1], w_whole[1], w_send.at[1], w_recv.at[1], dev_yr).wait_recv()
    w_b = remote(w_half(y_right, 1), w_half(y_right, 1), w_send.at[3], w_recv.at[3], dev_yl)
    w_b.start()
    prepare()

    def wait_b(o, _):
        src = lax.rem(s + o, NS)
        remote(pbuf.at[src], pbuf.at[src], b_send.at[o], b_recv.at[src], (src, e)).wait_recv()
        return 0

    lax.fori_loop(1, NS, wait_b, 0)
    for d in range(NS):
        piece = pbuf[d].astype(f32)
        for r in range(4):
            inc[pl.ds(4 * d + r, HEADS, stride=HD), :] = piece[8 * r : 8 * r + 8]
    for h in range(HEADS):
        cols = slice(h * HD, (h + 1) * HD)
        out = loc[:, cols] + jnp.dot(
            qd[:, cols], inc[cols, :].astype(bf16), preferred_element_type=f32
        )
        mean = jnp.mean(out * out, axis=1, keepdims=True)
        gate = 1.0 / (1.0 + jnp.exp(-g_ref[:, cols].astype(f32)))
        act[z, :, cols] = (out * lax.rsqrt(mean + epsilon) * gain_ref[0:1, cols] * gate).astype(
            bf16
        )

    z_right, z_left = lax.rem(z + 1, NZ), lax.rem(z + NZ - 1, NZ)
    dev_zr, dev_zl = (z_right * NY + y, e), (z_left * NY + y, e)

    def at(k):
        return lax.rem(z + k + NZ, NZ)

    def ring(k):
        own_r, own_l = at(1 - k), at(k - 1)
        if k < 4:
            src_r, src_l = act.at[own_r], act.at[own_l]
        else:
            src_r, src_l = act.at[own_r, 0:64], act.at[own_l, 64:128]
        right = remote(src_r, src_r, r_send.at[2 * k - 2], r_recv.at[2 * k - 2], dev_zr)
        left = remote(src_l, src_l, r_send.at[2 * k - 1], r_recv.at[2 * k - 1], dev_zl)
        right.start()
        left.start()
        return right, left

    def ring_wait(k):
        got_r, got_l = at(-k), at(k)
        if k < 4:
            dst_r, dst_l = act.at[got_r], act.at[got_l]
        else:
            dst_r, dst_l = act.at[got_r, 0:64], act.at[got_l, 64:128]
        remote(dst_r, dst_r, r_send.at[2 * k - 2], r_recv.at[2 * k - 2], dev_zl).wait_recv()
        remote(dst_l, dst_l, r_send.at[2 * k - 1], r_recv.at[2 * k - 1], dev_zr).wait_recv()

    sibling = (s, e + 1 - 2 * c)
    mine = pl.ds(pl.multiple_of(c * 384, 384), 384)
    other = pl.ds(pl.multiple_of((1 - c) * 384, 384), 384)

    def product(k):
        blk = at(k)
        pb[blk] = lax.dot_general(
            wcat[...], act[blk], (((1,), (1,)), ((), ())), preferred_element_type=f32
        ).astype(bf16)
        remote(
            pb.at[blk, other], sb.at[blk], sb_send.at[blk], sb_recv.at[blk], sibling
        ).start()

    def pass_on(k):
        blk = at(k)
        remote(
            pb.at[blk, other], sb.at[blk], sb_send.at[blk], sb_recv.at[blk], sibling
        ).wait_recv()
        both = (pb[blk, mine].astype(f32) + sb[blk].astype(f32)).astype(bf16)
        qb[blk] = both

        @pl.when(blk != e)
        def _():
            remote(qb.at[blk], rs.at[e], rs_send.at[blk], rs_recv.at[e], (s, blk)).start()

        @pl.when(blk == e)
        def _():
            rs[e] = both

    sends = [ring(1)]
    wl.wait()
    remote(
        w_half(y_far, 0), w_half(y_far, 0), w_send.at[2], w_recv.at[2], dev_yl
    ).wait_recv()
    remote(
        w_half(y_far, 1), w_half(y_far, 1), w_send.at[3], w_recv.at[3], dev_yr
    ).wait_recv()
    product(0)
    ring_wait(1)
    sends.append(ring(2))
    product(-1)
    product(1)
    pass_on(0)
    ring_wait(2)
    sends.append(ring(3))
    product(-2)
    product(2)
    pass_on(-1)
    pass_on(1)
    ring_wait(3)
    sends.append(ring(4))
    product(-3)
    product(3)
    pass_on(-2)
    pass_on(2)
    ring_wait(4)
    product(4)
    pass_on(-3)
    pass_on(3)
    pass_on(4)

    def wait_rs(o, _):
        src = lax.rem(e + o, NE)
        remote(rs.at[src], rs.at[src], rs_send.at[src], rs_recv.at[src], (s, src)).wait_recv()
        return 0

    lax.fori_loop(1, NE, wait_rs, 0)
    for core in range(2):
        acc = rs[core].astype(f32)
        for x in range(1, 4):
            acc += rs[2 * x + core].astype(f32)
        ysend[core * 384 : core * 384 + 384, :] = acc.astype(bf16)

    def send_y(o):
        peer = lax.rem(y + o, NY)
        return remote(
            ysend.at[cols_of(peer, 0, COLS)], yrecv.at[y], y_send.at[o], y_recv.at[y],
            (z * NY + peer, e),
        )

    for o in range(1, NY):
        send_y(o).start()
    yrecv[y] = ysend[cols_of(y, 0, COLS), :]
    for o in range(1, NY):
        src = lax.rem(y + o, NY)
        remote(
            yrecv.at[src], yrecv.at[src], y_send.at[o], y_recv.at[src], (z * NY + src, e)
        ).wait_recv()
    for i in range(NY):
        cols = slice(i * TOK, (i + 1) * TOK)
        after[:, cols] = res_ref[:, cols].astype(f32) + yrecv[i].astype(f32)

    experts()

    def drain_state(o, _):
        peer = lax.rem(s + o, NS)
        remote(ub.at[peer], rbuf.at[s], a_send.at[o], a_recv.at[s], (peer, e)).wait_send()
        remote(pref.at[peer], pbuf.at[s], b_send.at[o], b_recv.at[s], (peer, e)).wait_send()
        return 0

    lax.fori_loop(1, NS, drain_state, 0)
    for copy in (w_r, w_l, w_f, w_b):
        copy.wait_send()
    for right, left in sends:
        right.wait_send()
        left.wait_send()
    for blk in range(NZ):
        remote(
            pb.at[blk, other], sb.at[blk], sb_send.at[blk], sb_recv.at[blk], sibling
        ).wait_send()

        @pl.when(blk != e)
        def _():
            remote(qb.at[blk], rs.at[e], rs_send.at[blk], rs_recv.at[e], (s, blk)).wait_send()

    for o in range(1, NY):
        send_y(o).wait_send()
    drain_experts()


def local(
    residual, query, key_in, value_in, gate_in, log_decay, state_in, attn_gain, w_out,
    moe_gain, router, w_gate, w_up, w_down, expert_ids, keep_counts,
):
    vmem = pl.BlockSpec(memory_space=pltpu.VMEM)
    hbm = pl.BlockSpec(memory_space=pl.ANY)
    dma = pltpu.SemaphoreType.DMA
    wide = HEADS * HD
    V = pltpu.VMEM
    out, final = pl.pallas_call(
        layer_kernel,
        out_shape=(
            jax.ShapeDtypeStruct((COLS, NY * TOK), bf16),
            jax.ShapeDtypeStruct((HEADS, 4, HD), f32),
        ),
        in_specs=[vmem] * 7 + [hbm] + [vmem] * 5 + [hbm] * 3,
        out_specs=(vmem, vmem),
        scratch_shapes=[
            V((TOK, HD), f32), V((TOK, HD), f32), V((HD, TOK), f32), V((TOK, wide), bf16),
            V((wide, HD), f32), V((NS, 48, HD), bf16), V((NS, 48, HD), bf16),
            V((NS, 32, HD), bf16), V((NS, 32, HD), bf16), V((wide, HD), f32),
            V((TOK, wide), f32), V((TOK, wide), bf16),
            V((NY * COLS, wide), bf16), V((NZ, TOK, wide), bf16),
            V((NZ, NY * COLS, TOK), bf16), V((NZ, 384, TOK), bf16), V((NZ, 384, TOK), bf16),
            V((NE, 384, TOK), bf16), V((NY * COLS, TOK), bf16), V((NY, COLS, TOK), bf16),
            V((COLS, NY * TOK), f32), V((1024, 512), bf16), V((1024, 512), bf16),
            V((3, 1024, 384), bf16), V((NE, 8, 128), f32), V((NS, 8, 128), f32),
            V((NE, 8, 128), f32), V((NE, 8, 128), f32),
            V((NE, 64, 128), bf16), V((NE, 64, 128), bf16),
            V((NE, 64, 128), bf16), V((NE, 64, 128), bf16),
            V((NZ, NY, 192, 128), bf16), V((NZ, NY, 288, 128), bf16), V((NZ, NY, 192, 128), bf16),
            V((NZ, NY, 288, 128), bf16), V((NZ, NY, 432, 128), bf16), V((NZ, NY, 288, 128), bf16),
            V((288, D), bf16), V((288, D), bf16), V((COLS, 9216), bf16),
            V((288, 384), f32), V((288, 384), f32),
            dma(()), dma((4,)), dma((4,)), dma((NS,)), dma((NS,)), dma((NS,)), dma((NS,)),
            dma((8,)), dma((8,)), dma((8,)), dma((8,)), dma((8,)), dma((8,)), dma((4,)), dma((4,)),
            dma((3,)), dma((8,)), dma((8,)), dma((NS,)), dma((NS,)), dma((8,)), dma((8,)),
            dma((8,)), dma((8,)), dma((8,)), dma((8,)), dma((2, 52)), dma((2, 52)),
        ],
        compiler_params=pltpu.CompilerParams(
            collective_id=0, has_side_effects=True, vmem_limit_bytes=62 * 1024 * 1024
        ),
        name="layer",
    )(
        query, key_in, value_in, gate_in, log_decay.T, state_in.reshape(wide, HD),
        attn_gain.reshape(1, wide), w_out.T, residual.T, moe_gain.reshape(1, COLS), router.T,
        expert_ids.T, keep_counts.reshape(1, 32), w_gate[0], w_up[0], w_down[0].T,
    )
    return out.T, final


def solution(mesh):
    in_specs = (
        P("exp", "seq"),
        P("seq", "exp"),
        P("seq", "exp"),
        P("seq", "exp"),
        P("seq", "exp"),
        P("seq", "exp"),
        P("exp", None, None),
        P("exp"),
        P("exp", "seq"),
        P("seq"),
        P("seq", None),
        P("exp", "seq", None),
        P("exp", "seq", None),
        P("exp", None, "seq"),
        P("exp", None),
        P(),
    )
    out_specs = (P("exp", "seq"), P("exp", "seq", None))
    return jax.shard_map(local, mesh=mesh, in_specs=in_specs, out_specs=out_specs, check_vma=False)
```

time: 471 us -> 188 us (0.40)
  waiting for transfers between devices: 174 us -> 0 us
  Pallas kernels: 68 us -> 184 us
  blocking collectives: 103 us -> 0 us
  local copies, waits for them, and re-layouts: 51.1 us -> 2.94 us
  other arithmetic: 33.5 us -> 0 us
  matrix products: 18.8 us -> 0 us
  between operations: 14.8 us -> 0.65 us
  starting transfers between devices: 5.49 us -> 0 us
    all_gather x2 -> x0, waiting for transfers between devices: 169 us -> none  [the longest x1 92.3 us: local(): lax.all_gather(hidden, 'seq', axis=1, tiled=True)]
    pallas_call x1, Pallas kernels: 68 us -> 184 us  [local(): pl.pallas_call(layer_kernel, out_shape=(jax.ShapeDtypeStruct((COLS, NY *...]
    psum x1 -> x0, blocking collectives: 58.7 us -> none  [local(): lax.psum((jnp.sum(after_attn * after_attn, axis=1), chosen_part), 'seq')]
    unnamed x1 -> x0, blocking collectives: 25.2 us -> none
    unnamed x45 -> x2, local copies, waits for them, and re-layouts: 27.3 us -> 2.94 us
    all_to_all x1 -> x0, blocking collectives: 18.8 us -> none  [local(): lax.all_to_all(sending, 'exp', split_axis=0, concat_axis=1, tiled=True)]
    dot_general x5 -> x0, matrix products: 17.4 us -> none  [the longest x1 6.76 us: local(): jnp.dot(lax.all_gather(hidden, 'seq', axis=1, tiled=True), down_rows, pre...]
    unnamed x3 -> x0, other arithmetic: 12.7 us -> none
  transfers between devices with their start and end apart: 3 -> 0, of which waited for: 3 -> 0; matrix products, arithmetic and copies ran while one was open for 0% -> 0% of each run, Pallas kernels for 0% -> 0%
where the time goes in v2:
time: 188 us
  Pallas kernels  184 us (98%)
  local copies, waits for them, and re-layouts  2.94 us (2%)
    pallas_call x1, Pallas kernels, local(): pl.pallas_call(layer_kernel, out_shape=(jax.ShapeDtypeStruct((COLS, NY *...  184 us

profile of v2, /device:TPU:1, one launch (start us, length us, event | category | flops | bytes accessed | tf_op | source)
XLA Modules:
  0.0 187.5 jit_solution(14395574086544694547)
XLA Ops:
  0.6 183.9 %layer.1 = (bf16[192,512]{1,0:T(8,128)(2,1)}, f32[8,4,128]{2,1,0:T(4,128)}) custom-call(bf16[128,1024]{1,0:T(8,128)(2,1)} %q_ref.1, bf16[128,1024]{1,0:T(8,128)(2,1)} %k_ref.1, bf16[128,1024]{1,0:T(8,128)(2,1)} %v_ref.1, bf16[128,1024]{1,0:T(8,128)(2,1)} %g_ref.1, f32[8,128]{1,0:T(8,128)} %bitcast.23, f32[1024,128]{1,0:T(8,128)} %bitcast.18, ...), custom_call_target="tpu_custom_call" | custom-call | tf_op jit(solution)/shard_map/layer/pallas_call | solution.py:702
  184.6 1.6 copy.20
  186.2 1.3 copy.21
